TPU v7x, 32 devices: a whole 2x2x4 slice. The times are simulated.
32 devices in a mesh: section: 2 (over x), seq: 4 (over z), tensor: 4 (over y, core).
Axes of the slice: x: 2, y: 2, z: 4, core: 2. Of those that a mesh axis runs over, the one named last changes fastest.
Arguments:
- q_mant: bfloat16 [2, 256, 16384], P('section', 'seq', 'tensor'), may hold values from -32 to 32
- q_scale: int32 [2, 256, 512], P('section', 'seq', 'tensor'), may hold values from -2 to 2
- key_mantissa_block: bfloat16 [2, 256, 1024], P('section', 'seq', 'tensor'), may hold values from -32 to 32
- key_exponent_scale: int32 [2, 256, 32], P('section', 'seq', 'tensor'), may hold values from -2 to 2
- value_mantissa_block: bfloat16 [2, 256, 1024], P('section', 'seq', 'tensor'), may hold values from -6 to 6
- value_exponent_scale: int32 [2, 256, 32], P('section', 'seq', 'tensor'), may hold values from -1 to 1
- cached_key_rows: bfloat16 [2, 8, 512, 128], P('section', 'tensor', 'seq'), may hold values from -12 to 12
- cached_value_rows: bfloat16 [2, 8, 512, 128], P('section', 'tensor', 'seq'), may hold values from -8 to 8
- start: int32 [2], P('section'), may hold values from 256 to 512, as said below
Outputs:
- attended: bfloat16 [2, 256, 16384], P('section', 'seq', 'tensor')
Inputs may be any that keep to these rules, and one draw needn't show every extreme that they name: The first start[s] cached positions of section s hold earlier tokens; the cache of some section is full in every draw.
All inputs are finite; a program needn't handle non-finite values.
Results may differ from a plain program's by a relative error of at most 0.0023.
Values may be sent and summed in bfloat16 or wider, within the bound.
No kernel may reach another device: no remote copies, remote signals or barrier semaphores. Data moves between devices by JAX's collectives and lax.ppermute only.
A program may use at most 64 MiB of HBM per device.

v0:
```python
import math
import jax
import jax.numpy as jnp
from jax import lax
from jax.sharding import PartitionSpec as P


def shifted(block, axis, distance):
    devices = range(lax.axis_size(axis))
    route = [((i - distance) % len(devices), i) for i in devices]
    return lax.ppermute(block, axis, route)


def decode_mantissas(mantissa, exponent):
    row_count, feature_count = mantissa.shape
    blocks = mantissa.astype(jnp.float32).reshape(row_count, feature_count // 32, 32)
    factor = jnp.exp2(exponent.astype(jnp.float32))[:, :, None]
    return (blocks * factor).reshape(row_count, feature_count).astype(jnp.bfloat16)


def attend(running, queries, section_key_rows, section_value_rows, key_start, from_cache, limit):
    head_count, tokens, head_size = queries.shape
    key_count = section_key_rows.shape[1]
    block_rows = min(512, tokens)
    inv_root = 1.0 / math.sqrt(head_size)
    key_first = jnp.asarray(key_start, jnp.int32)
    key_index = lax.iota(jnp.int32, key_count)

    def one_block(number, running):
        first_row = number * block_rows

        def update(running):
            row_max, row_total, row_sum = running
            query_block = lax.dynamic_slice_in_dim(queries, first_row, block_rows, 1)
            scores = (
                jnp.einsum(
                    "hqd,hkd->hqk",
                    query_block,
                    section_key_rows,
                    preferred_element_type=jnp.float32,
                )
                * inv_root
            )
            if from_cache:
                allowed = jnp.broadcast_to((key_index < limit)[None, None, :], scores.shape)
            else:
                query_index = first_row + lax.iota(jnp.int32, block_rows)
                allowed = jnp.broadcast_to(
                    (key_index[None, :] <= query_index[:, None])[None], scores.shape
                )
            scores = jnp.where(allowed, scores, -1e30)
            old_max = lax.dynamic_slice_in_dim(row_max, first_row, block_rows, 1)
            new_max = jnp.maximum(old_max, jnp.max(scores, axis=2))
            weights = jnp.where(allowed, jnp.exp(scores - new_max[:, :, None]), 0.0)
            factor = jnp.exp(old_max - new_max)
            old_total = lax.dynamic_slice_in_dim(row_total, first_row, block_rows, 1)
            new_total = old_total * factor + jnp.sum(weights, axis=2)
            product = jnp.einsum(
                "hqk,hkd->hqd",
                weights.astype(jnp.bfloat16),
                section_value_rows,
                preferred_element_type=jnp.float32,
            )
            old_sum = lax.dynamic_slice_in_dim(row_sum, first_row, block_rows, 1)
            new_sum = old_sum * factor[:, :, None] + product
            return (
                lax.dynamic_update_slice_in_dim(row_max, new_max, first_row, 1),
                lax.dynamic_update_slice_in_dim(row_total, new_total, first_row, 1),
                lax.dynamic_update_slice_in_dim(row_sum, new_sum, first_row, 1),
            )

        if from_cache:
            visible = key_first < limit
        else:
            visible = key_first <= first_row + block_rows - 1
        return lax.cond(visible, update, lambda unchanged: unchanged, running)

    return lax.fori_loop(0, tokens // block_rows, one_block, running)


def body(
    q_mant,
    q_scale,
    key_mantissa_block,
    key_exponent_scale,
    value_mantissa_block,
    value_exponent_scale,
    cached_key_rows,
    cached_value_rows,
    start,
):
    arrived = shifted(
        (
            q_mant[0],
            key_mantissa_block[0],
            value_mantissa_block[0],
            q_scale[0].astype(jnp.bfloat16),
            key_exponent_scale[0].astype(jnp.bfloat16),
            value_exponent_scale[0].astype(jnp.bfloat16),
        ),
        "section",
        1,
    )
    row_count = q_mant.shape[1]
    kv_here = cached_key_rows.shape[1]
    head_size = cached_key_rows.shape[3]
    queries = decode_mantissas(arrived[0], arrived[3]).reshape(row_count, -1, head_size)
    section_key_rows = decode_mantissas(arrived[1], arrived[4]).reshape(
        row_count, kv_here, head_size
    )
    section_value_rows = decode_mantissas(arrived[2], arrived[5]).reshape(
        row_count, kv_here, head_size
    )
    heads_here = queries.shape[1]
    query_group_width = heads_here // kv_here
    seq_count = lax.axis_size("seq")
    local_heads = heads_here // seq_count
    tokens = row_count * seq_count
    limit = start[0]
    mine = lax.all_to_all(queries, "seq", split_axis=1, concat_axis=0, tiled=True)
    query_block = jnp.transpose(mine, (1, 0, 2))
    running = (
        jnp.full((local_heads, tokens), -1e30, jnp.float32),
        jnp.zeros((local_heads, tokens), jnp.float32),
        jnp.zeros((local_heads, tokens, head_size), jnp.float32),
    )
    head_ids = lax.axis_index("seq") * local_heads + lax.iota(jnp.int32, local_heads)
    kv_ids = head_ids // query_group_width
    pieces = (
        lax.all_gather(cached_key_rows[0], "seq", axis=1, tiled=True),
        lax.all_gather(cached_value_rows[0], "seq", axis=1, tiled=True),
    )
    running = attend(
        running,
        query_block,
        jnp.take(pieces[0], kv_ids, axis=0),
        jnp.take(pieces[1], kv_ids, axis=0),
        jnp.int32(0),
        True,
        limit,
    )
    pieces = (
        lax.all_gather(section_key_rows, "seq", axis=0, tiled=True),
        lax.all_gather(section_value_rows, "seq", axis=0, tiled=True),
    )
    picked_keys = jnp.swapaxes(jnp.take(pieces[0], kv_ids, axis=1), 0, 1)
    picked_values = jnp.swapaxes(jnp.take(pieces[1], kv_ids, axis=1), 0, 1)
    running = attend(running, query_block, picked_keys, picked_values, jnp.int32(0), False, limit)
    row_max, row_total, row_sum = running
    finished = (row_sum / row_total[:, :, None]).astype(jnp.bfloat16)
    finished = jnp.transpose(finished, (1, 0, 2))
    returned = lax.all_to_all(finished, "seq", split_axis=0, concat_axis=1, tiled=True)
    return returned.reshape(1, row_count, heads_here * head_size)


def solution(mesh):
    return jax.shard_map(
        body,
        mesh=mesh,
        in_specs=(
            P("section", "seq", "tensor"),
            P("section", "seq", "tensor"),
            P("section", "seq", "tensor"),
            P("section", "seq", "tensor"),
            P("section", "seq", "tensor"),
            P("section", "seq", "tensor"),
            P("section", "tensor", "seq", None),
            P("section", "tensor", "seq", None),
            P("section"),
        ),
        out_specs=P("section", "seq", "tensor"),
        check_vma=False,
    )
```

profile of v0, /device:TPU:0, one launch (start us, length us, event | category | flops | bytes accessed | tf_op | source)
XLA Modules:
  0.0 120.3 jit_solution(3274771388179172553)
XLA Ops:
  0.0 3.0 %collective-permute-start = (bf16[64,4096]{1,0:T(8,128)(2,1)}, bf16[64,4096]{1,0:T(8,128)(2,1)S(1)}, u32[]{:S(2)}, u32[]{:S(2)}) collective-permute-start(bf16[64,4096]{1,0:T(8,128)(2,1)} %bitcast.60), channel_id=1, source_target_pairs={{16,0},{0,16},{17,1},{1,17},{18,2},{2,18},{19,3},{3,19},{20,4},{4,... | collective-permute-start | bytes 1572872 | tf_op jit(solution)/shard_map/ppermute | solution.py:11
  3.0 0.8 convert_bitcast_fusion
  3.7 0.0 collective-permute-start.1
  3.7 0.9 copy.39
  4.6 2.1 %collective-permute-start.2 = (bf16[64,256]{0,1:T(8,128)(2,1)S(1)}, bf16[64,256]{0,1:T(8,128)(2,1)S(1)}, u32[]{:S(2)}, u32[]{:S(2)}) collective-permute-start(bf16[64,256]{0,1:T(8,128)(2,1)S(1)} %bitcast.59), channel_id=1, source_target_pairs={{16,0},{0,16},{17,1},{1,17},{18,2},{2,18},{19,3},{3,19},{20,4},{4,... | collective-permute-start | bytes 98312 | tf_op jit(solution)/shard_map/ppermute | solution.py:11
  6.7 0.7 convert_bitcast_fusion.2
  7.4 0.0 collective-permute-start.3
  7.4 0.9 copy.42
  8.3 2.1 %collective-permute-start.4 = (bf16[64,256]{0,1:T(8,128)(2,1)S(1)}, bf16[64,256]{0,1:T(8,128)(2,1)S(1)}, u32[]{:S(2)}, u32[]{:S(2)}) collective-permute-start(bf16[64,256]{0,1:T(8,128)(2,1)S(1)} %bitcast.58), channel_id=1, source_target_pairs={{16,0},{0,16},{17,1},{1,17},{18,2},{2,18},{19,3},{3,19},{20,4},{4,... | collective-permute-start | bytes 98312 | tf_op jit(solution)/shard_map/ppermute | solution.py:11
  10.4 0.7 convert_bitcast_fusion.1
  11.1 5.2 %collective-permute-done.1 = bf16[64,128]{1,0:T(8,128)(2,1)S(1)} collective-permute-done((bf16[64,128]{1,0:T(8,128)(2,1)S(1)}, bf16[64,128]{1,0:T(8,128)(2,1)S(1)}, u32[]{:S(2)}, u32[]{:S(2)}) %collective-permute-start.1) | collective-permute-done | bytes 16416 | tf_op jit(solution)/shard_map/ppermute | solution.py:11
  16.3 2.0 %collective-permute-start.5 = (bf16[64,8]{0,1:T(8,128)(2,1)S(1)}, bf16[64,8]{0,1:T(8,128)(2,1)S(1)}, u32[]{:S(2)}, u32[]{:S(2)}) collective-permute-start(bf16[64,8]{0,1:T(8,128)(2,1)S(1)} %convert_bitcast_fusion.1), channel_id=1, source_target_pairs={{16,0},{0,16},{17,1},{1,17},{18,2},{2,18},{19,3},{3,19},{20,4},{4,... | collective-permute-start | bytes 3080 | tf_op jit(solution)/shard_map/ppermute | solution.py:11
  18.3 0.1 copy.35
  18.4 0.5 copy.34
  18.9 0.0 copy-start.5
  18.9 0.0 copy-start.6
  19.0 0.2 fusion.17
  19.2 1.1 copy.36
  20.3 4.9 %all-to-all-start = ((bf16[64,32,128]{2,0,1:T(8,128)(2,1)}), bf16[64,32,128]{2,0,1:T(8,128)(2,1)S(1)}, u32[]{:S(2)}, u32[]{:S(2)}) async-start(bf16[64,32,128]{2,0,1:T(8,128)(2,1)} %copy.36), calls=%async_computation | async-start | bytes 1048576 | tf_op jit(solution)/shard_map/all_to_all | solution.py:120
  25.2 19.9 %all-gather = bf16[1,2,512,128]{3,2,1,0:T(8,128)(2,1)S(1)} all-gather(bf16[1,2,128,128]{3,2,1,0:T(8,128)(2,1)S(1)} %copy-done.5), channel_id=2, replica_groups=mesh['section'=2,'seq'=4,'tensor'=4] {'seq'}, dimensions={2}, use_global_device_ids=true | all-gather | bytes 327680 | tf_op jit(solution)/shard_map/all_gather | solution.py:130
  45.2 13.9 %all-gather.1 = bf16[1,2,512,128]{3,2,1,0:T(8,128)(2,1)S(1)} all-gather(bf16[1,2,128,128]{3,2,1,0:T(8,128)(2,1)S(1)} %copy-done.6), channel_id=3, replica_groups=mesh['section'=2,'seq'=4,'tensor'=4] {'seq'}, dimensions={2}, use_global_device_ids=true | all-gather | bytes 327680 | tf_op jit(solution)/shard_map/all_gather | solution.py:131
  59.1 0.7 gather_fusion
  59.8 1.7 %gather_fusion.1 = bf16[8,512,128]{2,1,0:T(8,128)(2,1)} fusion(bf16[2,512,128]{2,1,0:T(8,128)(2,1)S(1)} %bitcast.50, s32[1024]{0:T(1024)S(1)} %pad_clamp_fusion), kind=kCustom, calls=%fused_computation.2.clone | custom fusion | bytes 2097184 | tf_op jit(solution)/shard_map/jit(_take)/gather | solution.py:137
  62.2 1.1 broadcast_in_dim.78
  63.3 0.0 collective-permute-done.3
  63.3 0.1 copy.41
  63.4 13.6 %all_gather.14 = bf16[256,2,128]{2,0,1:T(8,128)(2,1)S(1)} all-gather(bf16[64,2,128]{2,0,1:T(8,128)(2,1)S(1)} %copy.41), channel_id=1, replica_groups=mesh['section'=2,'seq'=4,'tensor'=4] {'seq'}, dimensions={0}, use_global_device_ids=true | all-gather | bytes 163840 | tf_op jit(solution)/shard_map/all_gather | solution.py:143
  77.1 1.4 %gather_fusion.2 = bf16[8,256,128]{2,1,0:T(8,128)(2,1)} fusion(bf16[256,2,128]{2,0,1:T(8,128)(2,1)S(1)} %all_gather.14, s32[1024]{0:T(1024)S(1)} %pad_clamp_fusion), kind=kCustom, calls=%fused_computation.1.clone | custom fusion | bytes 1048608 | tf_op jit(solution)/shard_map/jit(_take)/gather | solution.py:146
  78.5 0.1 copy.44
  78.6 13.3 %all_gather.15 = bf16[256,2,128]{2,0,1:T(8,128)(2,1)S(1)} all-gather(bf16[64,2,128]{2,0,1:T(8,128)(2,1)S(1)} %copy.44), channel_id=1, replica_groups=mesh['section'=2,'seq'=4,'tensor'=4] {'seq'}, dimensions={0}, use_global_device_ids=true | all-gather | bytes 163840 | tf_op jit(solution)/shard_map/all_gather | solution.py:144
  92.0 1.4 %gather_fusion.3 = bf16[8,256,128]{2,1,0:T(8,128)(2,1)} fusion(bf16[256,2,128]{2,0,1:T(8,128)(2,1)S(1)} %all_gather.15, s32[1024]{0:T(1024)S(1)} %pad_clamp_fusion), kind=kCustom, calls=%fused_computation.3.clone | custom fusion | bytes 1048608 | tf_op jit(solution)/shard_map/jit(_take)/gather | solution.py:147
  93.4 1.6 %fusion.18 = (f32[8,256]{1,0:T(8,128)S(1)}, f32[8,256,256]{1,2,0:T(8,128)S(1)}) fusion(pred[256,256]{0,1:T(8,128)(4,1)S(1)} %iota_compare_fusion, bf16[8,256,128]{2,1,0:T(8,128)(2,1)S(1)} %bitcast.52, bf16[8,256,128]{2,1,0:T(8,128)(2,1)} %gather_fusion.2, pred[8]{0:T(512)(128)(4,1)S(1)} %compare_and_fusion), kind=kOutput, calls=%fused_computation.27 | convolution fusion | flops 136050688 | bytes 3219464 | tf_op jit(solution)/shard_map/while/body/eval_jaxpr/cond/branch_1_fun/hqd,hkd->hqk/dot_general | solution.py:36
  95.0 0.1 broadcast_in_dim.89
  95.2 5.8 %conditional.1 = ((f32[8,256]{1,0:T(8,128)S(1)}, f32[8,256]{1,0:T(8,128)S(1)}, f32[8,256,128]{2,1,0:T(8,128)})) conditional(s32[]{:T(128)} %convert_element_type.63, (f32[8,256]{1,0:T(8,128)S(1)}, f32[8,256]{1,0:T(8,128)S(1)}, f32[8,256,128]{2,1,0:T(8,128)}) %tuple.27, (s32[]{:T(128)}, s32[512]{0:T(512)S(1)}, ...), branch_computations={%region_0.2_spmd, %region_1.5_spmd.clone} | conditional | flops 552079872 | bytes 32116872 | solution.py:76
  95.2 0.7 broadcast_compare_fusion
  95.8 0.9 fusion
  96.7 1.3 %fusion.2 = f32[8,256]{1,0:T(8,128)S(1)} fusion(f32[8,256,512]{2,1,0:T(8,128)S(1)} %get-tuple-element.183, f32[8,256]{1,0:T(8,128)S(1)} %max.10, pred[512]{0:T(512)(128)(4,1)S(1)} %broadcast_compare_fusion), kind=kLoop, calls=%fused_computation.8 | loop fusion | flops 5240832 | bytes 4211200 | tf_op jit(solution)/shard_map/while/body/eval_jaxpr/cond/branch_1_fun/reduce_sum | solution.py:57
  98.0 0.2 copy-done.1
  98.3 1.7 %fusion.6 = f32[8,256,128]{2,1,0:T(8,128)S(1)} fusion(f32[8,256,512]{2,1,0:T(8,128)S(1)} %get-tuple-element.183, f32[8,256]{1,0:T(8,128)S(1)} %max.10, pred[512]{0:T(512)(128)(4,1)S(1)} %broadcast_compare_fusion, bf16[8,512,128]{2,1,0:T(8,128)(2,1)S(1)} %copy-done, bf16[8,512,128]{2,1,0:T(8,128)(2,1)S(1)} %get-tuple-element.164, ...), kind=kOutput, calls=%fused_computation.11 | convolution fusion | flops 274726912 | bytes 8405512 | tf_op jit(solution)/shard_map/while/body/eval_jaxpr/cond/branch_1_fun/hqk,hkd->hqd/dot_general | solution.py:58
  100.0 1.0 copy-done.2
  101.0 0.5 fusion.19
  101.5 0.7 copy-done.3
  102.2 0.1 copy-done.4
  102.3 1.4 %fusion.23 = bf16[256,8,128]{2,0,1:T(8,128)(2,1)S(1)} fusion(f32[8,256,256]{1,2,0:T(8,128)S(1)} %get-tuple-element.185, f32[8,256]{1,0:T(8,128)S(1)} %max.9, f32[8,256,128]{2,1,0:T(8,128)S(1)} %copy-done.3, pred[256,256]{0,1:T(8,128)(4,1)S(1)} %iota_compare_fusion, bf16[8,256,128]{2,1,0:T(8,128)(2,1)S(1)} %copy-done.4, ...), kind=kOutput, calls=%fused_computation.33 | convolution fusion | flops 138149888 | bytes 4284424 | tf_op jit(solution)/shard_map/while/body/eval_jaxpr/cond/branch_1_fun/hqk,hkd->hqd/dot_general | solution.py:58
  103.8 0.3 copy.46
  104.1 15.0 %all_to_all.33 = bf16[256,8,128]{2,1,0:T(8,128)(2,1)S(1)} all-to-all(bf16[256,8,128]{2,1,0:T(8,128)(2,1)S(1)} %copy.46), channel_id=1, replica_groups=mesh['section'=2,'seq'=4,'tensor'=4] {'seq'}, dimensions={0} | all-to-all | bytes 1048576 | tf_op jit(solution)/shard_map/all_to_all | solution.py:152
  119.2 0.1 copy.47
  119.3 1.0 reshape.69
  (31 shorter events, 0.2 us)
Async XLA Ops:
  0.0 18.4 %collective-permute-start = (bf16[64,4096]{1,0:T(8,128)(2,1)}, bf16[64,4096]{1,0:T(8,128)(2,1)S(1)}, u32[]{:S(2)}, u32[]{:S(2)}) collective-permute-start(bf16[64,4096]{1,0:T(8,128)(2,1)} %bitcast.60), channel_id=1, source_target_pairs={{16,0},{0,16},{17,1},{1,17},{18,2},{2,18},{19,3},{3,19},{20,4},{4,... | collective-permute-start | bytes 1572872 | tf_op jit(solution)/shard_map/ppermute | solution.py:11
  3.7 12.6 %collective-permute-start.1 = (bf16[64,128]{1,0:T(8,128)(2,1)S(1)}, bf16[64,128]{1,0:T(8,128)(2,1)S(1)}, u32[]{:S(2)}, u32[]{:S(2)}) collective-permute-start(bf16[64,128]{1,0:T(8,128)(2,1)S(1)} %convert_bitcast_fusion), channel_id=1, source_target_pairs={{16,0},{0,16},{17,1},{1,17},{18,2},{2,18},{19,3},{3,19},{20,4},{4,... | collective-permute-start | bytes 49160 | tf_op jit(solution)/shard_map/ppermute | solution.py:11
  4.6 58.7 %collective-permute-start.2 = (bf16[64,256]{0,1:T(8,128)(2,1)S(1)}, bf16[64,256]{0,1:T(8,128)(2,1)S(1)}, u32[]{:S(2)}, u32[]{:S(2)}) collective-permute-start(bf16[64,256]{0,1:T(8,128)(2,1)S(1)} %bitcast.59), channel_id=1, source_target_pairs={{16,0},{0,16},{17,1},{1,17},{18,2},{2,18},{19,3},{3,19},{20,4},{4,... | collective-permute-start | bytes 98312 | tf_op jit(solution)/shard_map/ppermute | solution.py:11
  7.4 55.9 %collective-permute-start.3 = (bf16[64,8]{0,1:T(8,128)(2,1)S(1)}, bf16[64,8]{0,1:T(8,128)(2,1)S(1)}, u32[]{:S(2)}, u32[]{:S(2)}) collective-permute-start(bf16[64,8]{0,1:T(8,128)(2,1)S(1)} %convert_bitcast_fusion.2), channel_id=1, source_target_pairs={{16,0},{0,16},{17,1},{1,17},{18,2},{2,18},{19,3},{3,19},{20,4},{4,... | collective-permute-start | bytes 3080 | tf_op jit(solution)/shard_map/ppermute | solution.py:11
  8.3 70.2 %collective-permute-start.4 = (bf16[64,256]{0,1:T(8,128)(2,1)S(1)}, bf16[64,256]{0,1:T(8,128)(2,1)S(1)}, u32[]{:S(2)}, u32[]{:S(2)}) collective-permute-start(bf16[64,256]{0,1:T(8,128)(2,1)S(1)} %bitcast.58), channel_id=1, source_target_pairs={{16,0},{0,16},{17,1},{1,17},{18,2},{2,18},{19,3},{3,19},{20,4},{4,... | collective-permute-start | bytes 98312 | tf_op jit(solution)/shard_map/ppermute | solution.py:11
  16.3 47.0 %collective-permute-start.5 = (bf16[64,8]{0,1:T(8,128)(2,1)S(1)}, bf16[64,8]{0,1:T(8,128)(2,1)S(1)}, u32[]{:S(2)}, u32[]{:S(2)}) collective-permute-start(bf16[64,8]{0,1:T(8,128)(2,1)S(1)} %convert_bitcast_fusion.1), channel_id=1, source_target_pairs={{16,0},{0,16},{17,1},{1,17},{18,2},{2,18},{19,3},{3,19},{20,4},{4,... | collective-permute-start | bytes 3080 | tf_op jit(solution)/shard_map/ppermute | solution.py:11
  18.9 6.2 %copy-start.5 = (bf16[1,2,128,128]{3,2,1,0:T(8,128)(2,1)S(1)}, bf16[1,2,128,128]{3,2,1,0:T(8,128)(2,1)}, u32[]{:S(2)}) copy-start(bf16[1,2,128,128]{3,2,1,0:T(8,128)(2,1)} %param.21) | copy-start | bytes 196612
  18.9 26.2 %copy-start.6 = (bf16[1,2,128,128]{3,2,1,0:T(8,128)(2,1)S(1)}, bf16[1,2,128,128]{3,2,1,0:T(8,128)(2,1)}, u32[]{:S(2)}) copy-start(bf16[1,2,128,128]{3,2,1,0:T(8,128)(2,1)} %param.22) | copy-start | bytes 196612
  20.3 73.1 %all-to-all-start = ((bf16[64,32,128]{2,0,1:T(8,128)(2,1)}), bf16[64,32,128]{2,0,1:T(8,128)(2,1)S(1)}, u32[]{:S(2)}, u32[]{:S(2)}) async-start(bf16[64,32,128]{2,0,1:T(8,128)(2,1)} %copy.36), calls=%async_computation | async-start | bytes 1048576 | tf_op jit(solution)/shard_map/all_to_all | solution.py:120
  96.7 1.3 %copy-start = (bf16[8,512,128]{2,1,0:T(8,128)(2,1)S(1)}, bf16[8,512,128]{2,1,0:T(8,128)(2,1)}, u32[]{:S(2)}) copy-start(bf16[8,512,128]{2,1,0:T(8,128)(2,1)} %get-tuple-element.165) | copy-start | bytes 3145732 | tf_op jit(solution)/shard_map/while/body/eval_jaxpr/cond
  96.7 1.5 %copy-start.1 = (f32[8,256,128]{2,1,0:T(8,128)S(1)}, f32[8,256,128]{2,1,0:T(8,128)}, u32[]{:S(2)}) copy-start(f32[8,256,128]{2,1,0:T(8,128)} %get-tuple-element.162) | copy-start | bytes 3145732 | tf_op jit(solution)/shard_map/while/body/eval_jaxpr/cond
  100.0 1.0 copy-start.2
  101.0 1.2 %copy-start.3 = (f32[8,256,128]{2,1,0:T(8,128)S(1)}, f32[8,256,128]{2,1,0:T(8,128)}, u32[]{:S(2)}) copy-start(f32[8,256,128]{2,1,0:T(8,128)} %get-tuple-element.147) | copy-start | bytes 3145732
  101.0 1.4 %copy-start.4 = (bf16[8,256,128]{2,1,0:T(8,128)(2,1)S(1)}, bf16[8,256,128]{2,1,0:T(8,128)(2,1)}, u32[]{:S(2)}) copy-start(bf16[8,256,128]{2,1,0:T(8,128)(2,1)} %gather_fusion.3) | copy-start | bytes 1572868
where the time goes:
time: 121 us; the launch traced here: 120 us
  blocking collectives  75.9 us (63%)
  starting transfers between devices  14 us (12%)
  local copies, waits for them, and re-layouts  13.7 us (11%)
  matrix products  5.59 us (5%)
  waiting for transfers between devices  5.23 us (4%)
  other arithmetic  4.94 us (4%)
    all_gather x1, blocking collectives, body(): lax.all_gather(cached_key_rows[0], 'seq', axis=1, tiled=True)  19.9 us
    all_to_all x1, blocking collectives, body(): lax.all_to_all(finished, 'seq', split_axis=0, concat_axis=1, tiled=True)  15 us
    all_gather x1, blocking collectives, body(): lax.all_gather(cached_value_rows[0], 'seq', axis=1, tiled=True)  13.9 us
    all_gather x1, blocking collectives, body(): lax.all_gather(section_key_rows, 'seq', axis=0, tiled=True)  13.6 us
    all_gather x1, blocking collectives, body(): lax.all_gather(section_value_rows, 'seq', axis=0, tiled=True)  13.3 us
    ppermute x6, starting transfers between devices, shifted(): return lax.ppermute(block, axis, route)  9.17 us
    ppermute x6, waiting for transfers between devices, shifted(): return lax.ppermute(block, axis, route)  5.23 us
    all_to_all x1, starting transfers between devices, body(): lax.all_to_all(queries, 'seq', split_axis=1, concat_axis=0, tiled=True)  4.87 us
  transfers between devices with their start and end apart: 7, of which 1 were waited for; matrix products, arithmetic and copies ran while one was open for 10% of the time, Pallas kernels for 0%

commit v1 on v0

--- a/solution.py
+++ b/solution.py
@@ -3,6 +3,18 @@
 import jax.numpy as jnp
 from jax import lax
 from jax.sharding import PartitionSpec as P
+
+
+def exchange_directly(x, axis, split, join):
+    ways, here = (lax.axis_size(axis), lax.axis_index(axis))
+    width = x.shape[split] // ways
+    turned = jnp.roll(x, -here * width, axis=split)
+    got = [lax.slice_in_dim(turned, 0, width, axis=split)]
+    for far in range(1, ways):
+        sent = lax.slice_in_dim(turned, far * width, (far + 1) * width, axis=split)
+        got.append(lax.ppermute(sent, axis, [(d, (d + far) % ways) for d in range(ways)]))
+    line = jnp.concatenate(got[::-1], axis=join)
+    return jnp.roll(line, (here + 1) * got[0].shape[join], axis=join)
 
 
 def shifted(block, axis, distance):
@@ -149,7 +161,7 @@
     row_max, row_total, row_sum = running
     finished = (row_sum / row_total[:, :, None]).astype(jnp.bfloat16)
     finished = jnp.transpose(finished, (1, 0, 2))
-    returned = lax.all_to_all(finished, "seq", split_axis=0, concat_axis=1, tiled=True)
+    returned = exchange_directly(finished, "seq", 0, 1)
     return returned.reshape(1, row_count, heads_here * head_size)
 
 

time: 121 us -> 108 us (0.89)
  blocking collectives: 75.9 us -> 59.6 us
  starting transfers between devices: 14 us -> 15.6 us
  waiting for transfers between devices: 5.23 us -> 6.76 us
    all_to_all x1 -> x0, blocking collectives: 15 us -> none  [body(): lax.all_to_all(finished, 'seq', split_axis=0, concat_axis=1, tiled=True)]
    ppermute x0 -> x3, waiting for transfers between devices: none -> 6.74 us  [exchange_directly(): lax.ppermute(sent, axis, [(d, (d + far) % ways) for d in range(ways)])]
    all_gather x1, blocking collectives: 19.9 us -> 14.4 us  [body(): lax.all_gather(cached_key_rows[0], 'seq', axis=1, tiled=True)]
    ppermute x6, waiting for transfers between devices: 5.23 us -> 0.02 us  [shifted(): return lax.ppermute(block, axis, route)]
    all_gather x1, blocking collectives: 13.9 us -> 18.4 us  [body(): lax.all_gather(cached_value_rows[0], 'seq', axis=1, tiled=True)]
    ppermute x0 -> x3, starting transfers between devices: none -> 3.44 us  [exchange_directly(): lax.ppermute(sent, axis, [(d, (d + far) % ways) for d in range(ways)])]
    ppermute x6, starting transfers between devices: 9.17 us -> 7.69 us  [shifted(): return lax.ppermute(block, axis, route)]
    unnamed x10 -> x15, local copies, waits for them, and re-layouts: 2.56 us -> 2.68 us
  transfers between devices with their start and end apart: 7 -> 10, of which waited for: 1 -> 2; matrix products, arithmetic and copies ran while one was open for 10% -> 12% of each run, Pallas kernels for 0% -> 0%
where the time goes in v1:
time: 108 us
  blocking collectives  59.6 us (55%)
  starting transfers between devices  15.6 us (14%)
  local copies, waits for them, and re-layouts  13.7 us (13%)
  waiting for transfers between devices  6.76 us (6%)
  matrix products  5.6 us (5%)
  other arithmetic  5.23 us (5%)
    all_gather x1, blocking collectives, body(): lax.all_gather(cached_value_rows[0], 'seq', axis=1, tiled=True)  18.4 us
    all_gather x1, blocking collectives, body(): lax.all_gather(cached_key_rows[0], 'seq', axis=1, tiled=True)  14.4 us
    all_gather x1, blocking collectives, body(): lax.all_gather(section_key_rows, 'seq', axis=0, tiled=True)  13.4 us
    all_gather x1, blocking collectives, body(): lax.all_gather(section_value_rows, 'seq', axis=0, tiled=True)  13.3 us
    ppermute x6, starting transfers between devices, shifted(): return lax.ppermute(block, axis, route)  7.69 us
    ppermute x3, waiting for transfers between devices, exchange_directly(): lax.ppermute(sent, axis, [(d, (d + far) % ways) for d in range(ways)])  6.74 us
    all_to_all x1, starting transfers between devices, body(): lax.all_to_all(queries, 'seq', split_axis=1, concat_axis=0, tiled=True)  4.52 us
    ppermute x3, starting transfers between devices, exchange_directly(): lax.ppermute(sent, axis, [(d, (d + far) % ways) for d in range(ways)])  3.44 us
  transfers between devices with their start and end apart: 10, of which 2 were waited for; matrix products, arithmetic and copies ran while one was open for 12% of the time, Pallas kernels for 0%

profile of v1, /device:TPU:0, one launch (start us, length us, event | category | flops | bytes accessed | tf_op | source)
XLA Modules:
  0.0 107.6 jit_solution(18225795082915073702)
XLA Ops:
  0.0 3.0 %collective-permute-start = (bf16[64,4096]{1,0:T(8,128)(2,1)}, bf16[64,4096]{1,0:T(8,128)(2,1)S(1)}, u32[]{:S(2)}, u32[]{:S(2)}) collective-permute-start(bf16[64,4096]{1,0:T(8,128)(2,1)} %bitcast.54), channel_id=1, source_target_pairs={{16,0},{0,16},{17,1},{1,17},{18,2},{2,18},{19,3},{3,19},{20,4},{4,... | collective-permute-start | bytes 1572872 | tf_op jit(solution)/shard_map/ppermute | solution.py:23
  3.0 0.8 convert_bitcast_fusion
  3.7 0.0 collective-permute-start.1
  3.7 0.9 copy.38
  4.6 2.1 %collective-permute-start.2 = (bf16[64,256]{0,1:T(8,128)(2,1)S(1)}, bf16[64,256]{0,1:T(8,128)(2,1)S(1)}, u32[]{:S(2)}, u32[]{:S(2)}) collective-permute-start(bf16[64,256]{0,1:T(8,128)(2,1)S(1)} %bitcast.53), channel_id=1, source_target_pairs={{16,0},{0,16},{17,1},{1,17},{18,2},{2,18},{19,3},{3,19},{20,4},{4,... | collective-permute-start | bytes 98312 | tf_op jit(solution)/shard_map/ppermute | solution.py:23
  6.7 0.7 convert_bitcast_fusion.2
  7.4 0.0 collective-permute-start.3
  7.4 0.9 copy.41
  8.3 2.1 %collective-permute-start.4 = (bf16[64,256]{0,1:T(8,128)(2,1)S(1)}, bf16[64,256]{0,1:T(8,128)(2,1)S(1)}, u32[]{:S(2)}, u32[]{:S(2)}) collective-permute-start(bf16[64,256]{0,1:T(8,128)(2,1)S(1)} %bitcast.52), channel_id=1, source_target_pairs={{16,0},{0,16},{17,1},{1,17},{18,2},{2,18},{19,3},{3,19},{20,4},{4,... | collective-permute-start | bytes 98312 | tf_op jit(solution)/shard_map/ppermute | solution.py:23
  10.4 0.7 convert_bitcast_fusion.1
  11.1 14.4 %all-gather = bf16[1,2,512,128]{3,2,1,0:T(8,128)(2,1)S(1)} all-gather(bf16[1,2,128,128]{3,2,1,0:T(8,128)(2,1)} %param.21), channel_id=2, replica_groups=mesh['section'=2,'seq'=4,'tensor'=4] {'seq'}, dimensions={2}, use_global_device_ids=true | all-gather | bytes 327680 | tf_op jit(solution)/shard_map/all_gather | solution.py:142
  25.5 0.5 collective-permute-start.5
  26.1 0.1 copy.34
  26.2 0.5 copy.33
  26.6 0.0 copy-start.5
  26.7 0.2 fusion.17
  26.9 1.1 %copy.35 = bf16[64,32,128]{2,0,1:T(8,128)(2,1)} copy(bf16[64,32,128]{0,2,1:T(8,128)(2,1)S(1)} %bitcast.46) | data formatting | bytes 1048576 | tf_op jit(solution)/shard_map/reshape | solution.py:119
  28.0 4.5 %all-to-all-start = ((bf16[64,32,128]{2,0,1:T(8,128)(2,1)}), bf16[64,32,128]{2,0,1:T(8,128)(2,1)S(1)}, u32[]{:S(2)}, u32[]{:S(2)}) async-start(bf16[64,32,128]{2,0,1:T(8,128)(2,1)} %copy.35), calls=%async_computation | async-start | bytes 1048576 | tf_op jit(solution)/shard_map/all_to_all | solution.py:132
  32.5 18.4 %all-gather.1 = bf16[1,2,512,128]{3,2,1,0:T(8,128)(2,1)S(1)} all-gather(bf16[1,2,128,128]{3,2,1,0:T(8,128)(2,1)S(1)} %copy-done.5), channel_id=3, replica_groups=mesh['section'=2,'seq'=4,'tensor'=4] {'seq'}, dimensions={2}, use_global_device_ids=true | all-gather | bytes 327680 | tf_op jit(solution)/shard_map/all_gather | solution.py:143
  51.0 0.7 gather_fusion
  51.7 1.7 %gather_fusion.1 = bf16[8,512,128]{2,1,0:T(8,128)(2,1)} fusion(bf16[2,512,128]{2,1,0:T(8,128)(2,1)S(1)} %bitcast.45, s32[1024]{0:T(1024)S(1)} %pad_clamp_fusion), kind=kCustom, calls=%fused_computation.2.clone | custom fusion | bytes 2097184 | tf_op jit(solution)/shard_map/jit(_take)/gather | solution.py:149
  54.1 1.1 %broadcast_in_dim.78 = f32[8,256,128]{2,1,0:T(8,128)} broadcast(f32[]{:T(128)} %constant.124.clone.1), dimensions={} | broadcast | bytes 1048580 | tf_op jit(solution)/shard_map/broadcast_in_dim | solution.py:137
  55.3 0.1 copy.40
  55.4 13.4 %all_gather.14 = bf16[256,2,128]{2,0,1:T(8,128)(2,1)S(1)} all-gather(bf16[64,2,128]{2,0,1:T(8,128)(2,1)S(1)} %copy.40), channel_id=1, replica_groups=mesh['section'=2,'seq'=4,'tensor'=4] {'seq'}, dimensions={0}, use_global_device_ids=true | all-gather | bytes 163840 | tf_op jit(solution)/shard_map/all_gather | solution.py:155
  68.7 1.4 %gather_fusion.2 = bf16[8,256,128]{2,1,0:T(8,128)(2,1)} fusion(bf16[256,2,128]{2,0,1:T(8,128)(2,1)S(1)} %all_gather.14, s32[1024]{0:T(1024)S(1)} %pad_clamp_fusion), kind=kCustom, calls=%fused_computation.1.clone | custom fusion | bytes 1048608 | tf_op jit(solution)/shard_map/jit(_take)/gather | solution.py:158
  70.2 0.1 copy.43
  70.3 13.3 %all_gather.15 = bf16[256,2,128]{2,0,1:T(8,128)(2,1)S(1)} all-gather(bf16[64,2,128]{2,0,1:T(8,128)(2,1)S(1)} %copy.43), channel_id=1, replica_groups=mesh['section'=2,'seq'=4,'tensor'=4] {'seq'}, dimensions={0}, use_global_device_ids=true | all-gather | bytes 163840 | tf_op jit(solution)/shard_map/all_gather | solution.py:156
  83.6 1.4 %gather_fusion.3 = bf16[8,256,128]{2,1,0:T(8,128)(2,1)} fusion(bf16[256,2,128]{2,0,1:T(8,128)(2,1)S(1)} %all_gather.15, s32[1024]{0:T(1024)S(1)} %pad_clamp_fusion), kind=kCustom, calls=%fused_computation.3.clone | custom fusion | bytes 1048608 | tf_op jit(solution)/shard_map/jit(_take)/gather | solution.py:159
  85.1 1.6 %fusion.18 = (f32[8,256]{1,0:T(8,128)S(1)}, f32[8,256,256]{1,2,0:T(8,128)S(1)}) fusion(pred[256,256]{0,1:T(8,128)(4,1)S(1)} %iota_compare_fusion, bf16[8,256,128]{2,1,0:T(8,128)(2,1)S(1)} %bitcast.47, bf16[8,256,128]{2,1,0:T(8,128)(2,1)} %gather_fusion.2, pred[8]{0:T(512)(128)(4,1)S(1)} %compare_and_fusion), kind=kOutput, calls=%fused_computation.27 | convolution fusion | flops 136050688 | bytes 3219464 | tf_op jit(solution)/shard_map/while/body/eval_jaxpr/cond/branch_1_fun/hqd,hkd->hqk/dot_general | solution.py:48
  86.7 0.1 broadcast_in_dim.89
  86.8 5.8 %conditional.1 = ((f32[8,256]{1,0:T(8,128)S(1)}, f32[8,256]{1,0:T(8,128)S(1)}, f32[8,256,128]{2,1,0:T(8,128)})) conditional(s32[]{:T(128)} %convert_element_type.63, (f32[8,256]{1,0:T(8,128)S(1)}, f32[8,256]{1,0:T(8,128)S(1)}, f32[8,256,128]{2,1,0:T(8,128)}) %tuple.27, (s32[]{:T(128)}, s32[512]{0:T(512)S(1)}, ...), branch_computations={%region_0.2_spmd, %region_1.5_spmd.clone} | conditional | flops 552079872 | bytes 32116872 | solution.py:88
  86.8 0.7 broadcast_compare_fusion
  87.5 0.9 fusion
  88.4 1.3 %fusion.2 = f32[8,256]{1,0:T(8,128)S(1)} fusion(f32[8,256,512]{2,1,0:T(8,128)S(1)} %get-tuple-element.183, f32[8,256]{1,0:T(8,128)S(1)} %max.10, pred[512]{0:T(512)(128)(4,1)S(1)} %broadcast_compare_fusion), kind=kLoop, calls=%fused_computation.8 | loop fusion | flops 5240832 | bytes 4211200 | tf_op jit(solution)/shard_map/while/body/eval_jaxpr/cond/branch_1_fun/reduce_sum | solution.py:69
  89.7 0.2 copy-done.1
  89.9 1.7 %fusion.6 = f32[8,256,128]{2,1,0:T(8,128)S(1)} fusion(f32[8,256,512]{2,1,0:T(8,128)S(1)} %get-tuple-element.183, f32[8,256]{1,0:T(8,128)S(1)} %max.10, pred[512]{0:T(512)(128)(4,1)S(1)} %broadcast_compare_fusion, bf16[8,512,128]{2,1,0:T(8,128)(2,1)S(1)} %copy-done, bf16[8,512,128]{2,1,0:T(8,128)(2,1)S(1)} %get-tuple-element.164, ...), kind=kOutput, calls=%fused_computation.11 | convolution fusion | flops 274726912 | bytes 8405512 | tf_op jit(solution)/shard_map/while/body/eval_jaxpr/cond/branch_1_fun/hqk,hkd->hqd/dot_general | solution.py:70
  91.6 1.0 copy-done.2
  92.6 0.5 fusion.19
  93.2 0.7 copy-done.3
  93.9 0.1 copy-done.4
  94.0 1.4 %fusion.23 = bf16[256,8,128]{2,0,1:T(8,128)(2,1)S(1)} fusion(f32[8,256,256]{1,2,0:T(8,128)S(1)} %get-tuple-element.188, f32[8,256]{1,0:T(8,128)S(1)} %max.9, f32[8,256,128]{2,1,0:T(8,128)S(1)} %copy-done.3, pred[256,256]{0,1:T(8,128)(4,1)S(1)} %iota_compare_fusion, bf16[8,256,128]{2,1,0:T(8,128)(2,1)S(1)} %copy-done.4, ...), kind=kOutput, calls=%fused_computation.33 | convolution fusion | flops 138149888 | bytes 4284424 | tf_op jit(solution)/shard_map/while/body/eval_jaxpr/cond/branch_1_fun/hqk,hkd->hqd/dot_general | solution.py:70
  95.4 0.3 fusion.30
  95.8 2.8 %collective-permute-start.6 = (bf16[64,8,128]{2,0,1:T(8,128)(2,1)S(1)}, bf16[64,8,128]{2,0,1:T(8,128)(2,1)S(1)}, u32[]{:S(2)}, u32[]{:S(2)}) collective-permute-start(bf16[64,8,128]{2,0,1:T(8,128)(2,1)S(1)} %get-tuple-element.186), channel_id=1, source_target_pairs={{0,12},{4,0},{8,4},{12,8},{1,13},{5,1},{9,5},{13,9},{2,14},{6,2},{... | collective-permute-start | bytes 393224 | tf_op jit(solution)/shard_map/ppermute | solution.py:15
  98.6 0.6 collective-permute-start.8
  99.2 1.9 %collective-permute-done.6 = bf16[64,8,128]{2,0,1:T(8,128)(2,1)S(1)} collective-permute-done((bf16[64,8,128]{2,0,1:T(8,128)(2,1)S(1)}, bf16[64,8,128]{2,0,1:T(8,128)(2,1)S(1)}, u32[]{:S(2)}, u32[]{:S(2)}) %collective-permute-start.6) | collective-permute-done | bytes 131104 | tf_op jit(solution)/shard_map/ppermute | solution.py:15
  101.1 4.8 %collective-permute-done.7 = bf16[64,8,128]{2,0,1:T(8,128)(2,1)S(1)} collective-permute-done((bf16[64,8,128]{2,0,1:T(8,128)(2,1)S(1)}, bf16[64,8,128]{2,0,1:T(8,128)(2,1)S(1)}, u32[]{:S(2)}, u32[]{:S(2)}) %collective-permute-start.7) | collective-permute-done | bytes 131104 | tf_op jit(solution)/shard_map/ppermute | solution.py:15
  106.2 0.3 copy.45
  106.6 1.0 reshape.68
  (44 shorter events, 0.4 us)
Async XLA Ops:
  0.0 26.2 %collective-permute-start = (bf16[64,4096]{1,0:T(8,128)(2,1)}, bf16[64,4096]{1,0:T(8,128)(2,1)S(1)}, u32[]{:S(2)}, u32[]{:S(2)}) collective-permute-start(bf16[64,4096]{1,0:T(8,128)(2,1)} %bitcast.54), channel_id=1, source_target_pairs={{16,0},{0,16},{17,1},{1,17},{18,2},{2,18},{19,3},{3,19},{20,4},{4,... | collective-permute-start | bytes 1572872 | tf_op jit(solution)/shard_map/ppermute | solution.py:23
  3.7 21.8 %collective-permute-start.1 = (bf16[64,128]{1,0:T(8,128)(2,1)S(1)}, bf16[64,128]{1,0:T(8,128)(2,1)S(1)}, u32[]{:S(2)}, u32[]{:S(2)}) collective-permute-start(bf16[64,128]{1,0:T(8,128)(2,1)S(1)} %convert_bitcast_fusion), channel_id=1, source_target_pairs={{16,0},{0,16},{17,1},{1,17},{18,2},{2,18},{19,3},{3,19},{20,4},{4,... | collective-permute-start | bytes 49160 | tf_op jit(solution)/shard_map/ppermute | solution.py:23
  4.6 50.6 %collective-permute-start.2 = (bf16[64,256]{0,1:T(8,128)(2,1)S(1)}, bf16[64,256]{0,1:T(8,128)(2,1)S(1)}, u32[]{:S(2)}, u32[]{:S(2)}) collective-permute-start(bf16[64,256]{0,1:T(8,128)(2,1)S(1)} %bitcast.53), channel_id=1, source_target_pairs={{16,0},{0,16},{17,1},{1,17},{18,2},{2,18},{19,3},{3,19},{20,4},{4,... | collective-permute-start | bytes 98312 | tf_op jit(solution)/shard_map/ppermute | solution.py:23
  7.4 47.8 %collective-permute-start.3 = (bf16[64,8]{0,1:T(8,128)(2,1)S(1)}, bf16[64,8]{0,1:T(8,128)(2,1)S(1)}, u32[]{:S(2)}, u32[]{:S(2)}) collective-permute-start(bf16[64,8]{0,1:T(8,128)(2,1)S(1)} %convert_bitcast_fusion.2), channel_id=1, source_target_pairs={{16,0},{0,16},{17,1},{1,17},{18,2},{2,18},{19,3},{3,19},{20,4},{4,... | collective-permute-start | bytes 3080 | tf_op jit(solution)/shard_map/ppermute | solution.py:23
  8.3 61.9 %collective-permute-start.4 = (bf16[64,256]{0,1:T(8,128)(2,1)S(1)}, bf16[64,256]{0,1:T(8,128)(2,1)S(1)}, u32[]{:S(2)}, u32[]{:S(2)}) collective-permute-start(bf16[64,256]{0,1:T(8,128)(2,1)S(1)} %bitcast.52), channel_id=1, source_target_pairs={{16,0},{0,16},{17,1},{1,17},{18,2},{2,18},{19,3},{3,19},{20,4},{4,... | collective-permute-start | bytes 98312 | tf_op jit(solution)/shard_map/ppermute | solution.py:23
  25.5 29.7 %collective-permute-start.5 = (bf16[64,8]{0,1:T(8,128)(2,1)S(1)}, bf16[64,8]{0,1:T(8,128)(2,1)S(1)}, u32[]{:S(2)}, u32[]{:S(2)}) collective-permute-start(bf16[64,8]{0,1:T(8,128)(2,1)S(1)} %convert_bitcast_fusion.1), channel_id=1, source_target_pairs={{16,0},{0,16},{17,1},{1,17},{18,2},{2,18},{19,3},{3,19},{20,4},{4,... | collective-permute-start | bytes 3080 | tf_op jit(solution)/shard_map/ppermute | solution.py:23
  26.6 5.9 %copy-start.5 = (bf16[1,2,128,128]{3,2,1,0:T(8,128)(2,1)S(1)}, bf16[1,2,128,128]{3,2,1,0:T(8,128)(2,1)}, u32[]{:S(2)}) copy-start(bf16[1,2,128,128]{3,2,1,0:T(8,128)(2,1)} %param.22) | copy-start | bytes 196612
  28.0 57.0 %all-to-all-start = ((bf16[64,32,128]{2,0,1:T(8,128)(2,1)}), bf16[64,32,128]{2,0,1:T(8,128)(2,1)S(1)}, u32[]{:S(2)}, u32[]{:S(2)}) async-start(bf16[64,32,128]{2,0,1:T(8,128)(2,1)} %copy.35), calls=%async_computation | async-start | bytes 1048576 | tf_op jit(solution)/shard_map/all_to_all | solution.py:132
  88.4 1.3 %copy-start = (bf16[8,512,128]{2,1,0:T(8,128)(2,1)S(1)}, bf16[8,512,128]{2,1,0:T(8,128)(2,1)}, u32[]{:S(2)}) copy-start(bf16[8,512,128]{2,1,0:T(8,128)(2,1)} %get-tuple-element.165) | copy-start | bytes 3145732 | tf_op jit(solution)/shard_map/while/body/eval_jaxpr/cond
  88.4 1.5 %copy-start.1 = (f32[8,256,128]{2,1,0:T(8,128)S(1)}, f32[8,256,128]{2,1,0:T(8,128)}, u32[]{:S(2)}) copy-start(f32[8,256,128]{2,1,0:T(8,128)} %get-tuple-element.162) | copy-start | bytes 3145732 | tf_op jit(solution)/shard_map/while/body/eval_jaxpr/cond
  91.6 1.0 copy-start.2
  92.6 1.2 %copy-start.3 = (f32[8,256,128]{2,1,0:T(8,128)S(1)}, f32[8,256,128]{2,1,0:T(8,128)}, u32[]{:S(2)}) copy-start(f32[8,256,128]{2,1,0:T(8,128)} %get-tuple-element.147) | copy-start | bytes 3145732
  92.6 1.4 %copy-start.4 = (bf16[8,256,128]{2,1,0:T(8,128)(2,1)S(1)}, bf16[8,256,128]{2,1,0:T(8,128)(2,1)}, u32[]{:S(2)}) copy-start(bf16[8,256,128]{2,1,0:T(8,128)(2,1)} %gather_fusion.3) | copy-start | bytes 1572868
  95.8 5.3 %collective-permute-start.6 = (bf16[64,8,128]{2,0,1:T(8,128)(2,1)S(1)}, bf16[64,8,128]{2,0,1:T(8,128)(2,1)S(1)}, u32[]{:S(2)}, u32[]{:S(2)}) collective-permute-start(bf16[64,8,128]{2,0,1:T(8,128)(2,1)S(1)} %get-tuple-element.186), channel_id=1, source_target_pairs={{0,12},{4,0},{8,4},{12,8},{1,13},{5,1},{9,5},{13,9},{2,14},{6,2},{... | collective-permute-start | bytes 393224 | tf_op jit(solution)/shard_map/ppermute | solution.py:15
  98.6 7.4 %collective-permute-start.7 = (bf16[64,8,128]{2,0,1:T(8,128)(2,1)S(1)}, bf16[64,8,128]{2,0,1:T(8,128)(2,1)S(1)}, u32[]{:S(2)}, u32[]{:S(2)}) collective-permute-start(bf16[64,8,128]{2,0,1:T(8,128)(2,1)S(1)} %get-tuple-element.185), channel_id=1, source_target_pairs={{0,8},{4,12},{8,0},{12,4},{1,9},{5,13},{9,1},{13,5},{2,10},{6,14},... | collective-permute-start | bytes 393224 | tf_op jit(solution)/shard_map/ppermute | solution.py:15
  98.6 7.4 %collective-permute-start.8 = (bf16[64,8,128]{2,0,1:T(8,128)(2,1)S(1)}, bf16[64,8,128]{2,0,1:T(8,128)(2,1)S(1)}, u32[]{:S(2)}, u32[]{:S(2)}) collective-permute-start(bf16[64,8,128]{2,0,1:T(8,128)(2,1)S(1)} %get-tuple-element.184), channel_id=1, source_target_pairs={{0,4},{4,8},{8,12},{12,0},{1,5},{5,9},{9,13},{13,1},{2,6},{6,10},{... | collective-permute-start | bytes 393224 | tf_op jit(solution)/shard_map/ppermute | solution.py:15
